TPU v7x, 32 devices: a whole 2x2x4 slice. The times are simulated.
32 devices in a mesh: dp: 4 (over z), row: 4 (over y, core), col: 2 (over x).
Axes of the slice: x: 2, y: 2, z: 4, core: 2. Of those that a mesh axis runs over, the one named last changes fastest.
Arguments:
- block_input: bfloat16 [8, 1792, 1024], P('dp', None, ('row', 'col')), may hold values from -45 to 45
- segment_ids: int32 [8, 1792], P('dp'), may hold values from 0 to 3, never falling along the last dimension, each value on 1 to 896 neighbouring positions
- out_grad: bfloat16 [8, 1792, 1024], P('dp', None, ('row', 'col')), may hold values from -6 to 6
- in_weight: bfloat16 [3, 1024, 1024], P(None, 'col', 'row'), may hold values from -0.1875 to 0.1875
- out_weight: bfloat16 [1024, 1024], P('row', 'col'), may hold values from -0.375 to 0.375
- gate_weight: bfloat16 [1024, 4608], P('col', 'row'), may hold values from -0.1875 to 0.1875
- up_weight: bfloat16 [1024, 4608], P('col', 'row'), may hold values from -0.1875 to 0.1875
- down_weight: bfloat16 [4608, 1024], P('row', 'col'), may hold values from -0.1875 to 0.1875
- conv_weight: bfloat16 [3, 1024], P(None, ('row', 'col')), may hold values from -3.5 to 3.5
- mixer_norm_gain: float32 [1024], replicated, may hold values from 0.5 to 1.5
- feedforward_norm_gain: float32 [1024], replicated, may hold values from 0.5 to 1.5
Outputs:
- block_output: bfloat16 [8, 1792, 1024], P('dp', None, ('row', 'col'))
- block_input_gradient: float32 [8, 1792, 1024], P('dp', None, ('row', 'col'))
- grad_in_weight: float32 [3, 1024, 1024], P(None, 'col', 'row')
- grad_out_weight: float32 [1024, 1024], P('row', 'col')
- grad_gate_weight: float32 [1024, 4608], P('col', 'row')
- grad_up_weight: float32 [1024, 4608], P('col', 'row')
- grad_down_weight: float32 [4608, 1024], P('row', 'col')
- grad_conv_weight: float32 [3, 1024], P(None, ('row', 'col'))
- mixer_gain_gradient: float32 [1024], P(('row', 'col'))
- feedforward_gain_gradient: float32 [1024], P(('row', 'col'))
Inputs may be any that keep to these rules, and one draw needn't show every extreme that they name: `segment_ids`: along each sequence the segment numbers never fall; a segment covers at most half of 1792 positions.
All inputs are finite; a program needn't handle non-finite values.
Results may differ from a plain program's by a relative error of at most 0.013.
Values may be sent and summed in bfloat16 or wider, within the bound.
No kernel may reach another device: no remote copies, remote signals or barrier semaphores. Data moves between devices by JAX's collectives and lax.ppermute only.
A program may use at most 256 MiB of HBM per device.

v0:
```python
import jax
import jax.numpy as jnp
from jax import lax
from jax.sharding import PartitionSpec as P


EPS = 1e-05
F32 = jnp.float32
BF16 = jnp.bfloat16


def contract(left, right, left_axis, right_axis):
    return lax.dot_general(
        left, right, (((left_axis,), (right_axis,)), ((), ())), preferred_element_type=F32
    )


def dot(left, right):
    return contract(left, right, 1, 0)


def dot_nt(left, right):
    return contract(left, right, 1, 1)


def dot_tn(left, right):
    return contract(left, right, 0, 0)


def rounded(values):
    return lax.reduce_precision(values, exponent_bits=8, mantissa_bits=7)


def in_order(first_is_mine, mine, other, axis):
    return jnp.where(
        first_is_mine,
        jnp.concatenate([mine, other], axis=axis),
        jnp.concatenate([other, mine], axis=axis),
    )


def swap_halves(values, axis):
    low, high = jnp.split(values, 2, axis=axis)
    return jnp.concatenate([high, low], axis=axis)


def rows_of(values, index, count):
    return lax.dynamic_slice_in_dim(values, index * count, count, axis=0)


def cols_of(values, index, count):
    return lax.dynamic_slice_in_dim(values, index * count, count, axis=1)


def after(values, *others):
    return lax.optimization_barrier((values, *others))[0]


def pad_rows(values, before, behind):
    return jnp.pad(values, ((before, behind), (0, 0)))


def to_col(values):
    size = lax.axis_size("col")
    return lax.ppermute(values, "col", [(i, size - 1 - i) for i in range(size)])


def to_core(values):
    size = lax.axis_size("row")
    return lax.ppermute(values, "row", [(i, i ^ 1) for i in range(size)])


def to_half(values):
    size = lax.axis_size("row")
    return lax.ppermute(values, "row", [(i, (i + size // 2) % size) for i in range(size)])


def line_sum(values, dtype, middle_after=(), outward_after=()):
    size = lax.axis_size("dp")
    place = lax.axis_index("dp")
    middle = size // 2
    keep = rounded if dtype == BF16 else (lambda v: v)
    total = values
    for step in range(middle - 1):
        pairs = [(step, step + 1), (size - 1 - step, size - 2 - step)]
        got = after(lax.ppermute(keep(total).astype(dtype), "dp", pairs), *middle_after)
        total = total + got.astype(F32)
    half = keep(total).astype(dtype)
    pairs = [(middle - 1, middle), (middle, middle - 1)]
    got = after(lax.ppermute(half, "dp", pairs), *outward_after)
    whole = keep(keep(total) + got.astype(F32)).astype(dtype)
    result = whole
    for step in range(middle - 1):
        pairs = [(middle - 1 - step, middle - 2 - step), (middle + step, middle + step + 1)]
        got = lax.ppermute(result, "dp", pairs)
        taker = (place == middle - 2 - step) | (place == middle + step + 1)
        result = jnp.where(taker, got, result)
    return result.astype(F32), half, whole


def body(
    block_input,
    segment_ids,
    out_grad,
    in_weight,
    out_weight,
    gate_weight,
    up_weight,
    down_weight,
    conv_weight,
    mixer_norm_gain,
    feedforward_norm_gain,
):
    seq_count, seq_length, own_width = block_input.shape
    if lax.axis_size("row") != 4 or lax.axis_size("col") != 2 or seq_count != 2 or lax.axis_size("dp") % 2:
        raise ValueError("unsupported mesh")
    row = lax.axis_index("row")
    col = lax.axis_index("col")
    part = row >> 1
    core = row & 1
    span = seq_length // 2
    home = span // 2
    width = mixer_norm_gain.shape[0]
    half_width = width // 2
    own_half_first = part == col
    core_low = core == 0
    part_low = part == 0
    col_low = col == 0

    def local_gain(gain):
        return jnp.concatenate(
            [
                lax.dynamic_slice_in_dim(gain, col * half_width, half_width),
                lax.dynamic_slice_in_dim(gain, (1 - col) * half_width, half_width),
            ]
        )

    def scatter_span(values):
        wide = 2 * own_width
        mine = cols_of(values, core, wide)
        got = to_core(cols_of(values, 1 - core, wide).astype(BF16)).astype(values.dtype)
        pair = in_order(core_low, mine, got, 0)
        mine = cols_of(pair, col, own_width)
        got = to_col(cols_of(pair, 1 - col, own_width).astype(BF16)).astype(values.dtype)
        return in_order(col_low, mine[None], got[None], 0)

    def local_features(mine, other):
        return jnp.concatenate(
            [jnp.where(own_half_first, mine, other), jnp.where(own_half_first, other, mine)], axis=1
        )

    def of_sequence(values, index):
        return lax.dynamic_index_in_dim(values, index, 0, keepdims=False)

    def gather_span(values, got):
        pair = in_order(col_low, of_sequence(values, col), got, 1)
        got = to_core(rows_of(pair, 1 - core, span))
        quad = in_order(core_low, rows_of(pair, core, span), got, 1)
        return quad, to_half(quad)

    input_got = to_col(of_sequence(block_input, 1 - col))
    input_half, input_other = gather_span(block_input, input_got)

    mixer_in = jnp.concatenate([in_weight, to_col(in_weight)], axis=1)
    mixer_in = jnp.concatenate([mixer_in, to_core(mixer_in)], axis=2)
    mixer_out = jnp.concatenate([out_weight, to_col(out_weight)], axis=1)
    mixer_out = jnp.concatenate([mixer_out, to_core(mixer_out)], axis=0)
    kernel = in_order(col_low, conv_weight, to_col(conv_weight), 1)
    kernel = jnp.concatenate([kernel, to_core(kernel)], axis=1).astype(F32)

    gate_got = to_col(gate_weight)
    cot_got = to_col(of_sequence(out_grad, 1 - col))
    up_got, down_got = to_col(up_weight), to_col(down_weight)
    hidden = gate_weight.shape[1]
    channels = in_weight.shape[2]

    gain_one = local_gain(mixer_norm_gain)
    gain_two = local_gain(feedforward_norm_gain)

    segments = lax.dynamic_index_in_dim(segment_ids, col, 0, keepdims=False)

    def same_as(lag):
        earlier = jnp.concatenate([jnp.full((lag,), -1, jnp.int32), segments[:-lag]])
        return rows_of(jnp.where(earlier == segments, 1.0, 0.0).astype(F32), core, span)[:, None]

    mask_one, mask_two = same_as(1), same_as(2)

    inputs = local_features(input_half, input_other).astype(F32)
    scale_one = lax.rsqrt(jnp.mean(inputs * inputs, axis=1, keepdims=True) + EPS)
    normed_one = (inputs * scale_one * gain_one).astype(BF16)
    projected = jnp.einsum("td,jdc->jtc", normed_one, mixer_in, preferred_element_type=F32)
    b_proj, c_proj, x_proj = projected[0], projected[1], projected[2]
    mixed_in = b_proj * x_proj
    edge_rows = 8
    rest = span - edge_rows
    before = jnp.where(core_low, 0.0, swap_halves(to_core(mixed_in[rest:]), 1))
    before_one = pad_rows(before[edge_rows - 1 :], 0, edge_rows - 1)
    before_two = pad_rows(before[edge_rows - 2 :], 0, edge_rows - 2)
    lag_one, lag_two = pad_rows(mixed_in[:-1], 1, 0), pad_rows(mixed_in[:-2], 2, 0)
    from_before = (
        kernel[1] * mask_one[:edge_rows] * before_one + kernel[2] * mask_two[:edge_rows] * before_two
    )
    conved = (
        kernel[0] * mixed_in
        + kernel[1] * mask_one * lag_one
        + kernel[2] * mask_two * lag_two
        + pad_rows(from_before, 0, rest)
    )
    gated_out = (c_proj * conved).astype(BF16)
    mixer_send = dot(rows_of(gated_out, 1 - part, home), mixer_out).astype(BF16)
    mixer_got = to_half(mixer_send)
    gate_all = jnp.concatenate([gate_weight, after(gate_got, mixer_send)], axis=0)
    gate_all = jnp.concatenate([gate_all, to_core(gate_all)], axis=1)
    resid_mid = rows_of(inputs, part, home) + dot(rows_of(gated_out, part, home), mixer_out) + mixer_got.astype(F32)

    scale_two = lax.rsqrt(jnp.mean(resid_mid * resid_mid, axis=1, keepdims=True) + EPS)
    hat_two = resid_mid * scale_two
    normed_own = (hat_two * gain_two).astype(BF16)
    normed_other = to_half(normed_own)
    cot_half, cot_other = gather_span(out_grad, after(cot_got, normed_own))
    normed_two = jnp.concatenate([normed_own, normed_other], axis=0)
    slot = jnp.where(own_half_first, 0, 1)
    resid_got = to_half(cols_of(resid_mid, 1 - slot, half_width).astype(BF16))
    gate_pre = dot(normed_two, gate_all)
    up_all = jnp.concatenate([up_weight, after(up_got, gate_pre)], axis=0)
    up_all = jnp.concatenate([up_all, to_core(up_all)], axis=1)
    up_pre = dot(normed_two, up_all)
    sigmoid = jax.nn.sigmoid(gate_pre)
    activated = (gate_pre * sigmoid * up_pre).astype(BF16)
    down_all = jnp.concatenate([down_weight, after(down_got, activated)], axis=1)
    down_all = jnp.concatenate([down_all, to_core(down_all)], axis=0)
    cot_span = local_features(cot_half, after(cot_other, activated))
    cotangent = jnp.concatenate([rows_of(cot_span, part, home), rows_of(cot_span, 1 - part, home)], axis=0)

    def finish(low, from_core, from_col):
        return low + from_core.astype(F32) + from_col.astype(F32)

    down_core = to_core(dot_tn(activated[:, hidden:], cotangent).astype(BF16))
    activated_mine = activated[:, :hidden]
    down_high = dot_tn(activated_mine, cotangent[:, half_width:])
    down_high = (down_high + down_core[:, half_width:].astype(F32)).astype(BF16)
    down_col = to_col(down_high)

    down_mine = cols_of(down_all, slot, half_width)
    down_other = cols_of(down_all, 1 - slot, half_width)
    output_send = dot(activated, down_other).astype(BF16)
    output_got = to_half(output_send)

    d_act = dot_nt(after(cotangent, down_high, output_send), down_all)
    d_up = (d_act * gate_pre * sigmoid).astype(BF16)
    d_gate = (d_act * up_pre * sigmoid * (1.0 + gate_pre * (1.0 - sigmoid))).astype(BF16)

    low, high = normed_two[:, :half_width], normed_two[:, half_width:]
    gate_core = to_core(dot_tn(normed_two, d_gate[:, hidden:]).astype(BF16))
    up_core = to_core(dot_tn(normed_two, d_up[:, hidden:]).astype(BF16))
    gate_mine, up_mine = d_gate[:, :hidden], d_up[:, :hidden]
    gate_high = dot_tn(high, gate_mine)
    gate_high = (gate_high + gate_core[half_width:].astype(F32)).astype(BF16)
    gate_col = to_col(gate_high)
    up_high = (dot_tn(high, up_mine) + up_core[half_width:].astype(F32)).astype(BF16)
    up_col = to_col(up_high)

    down_sum = finish(
        dot_tn(activated_mine, after(cotangent, up_high)[:, :half_width]),
        down_core[:, :half_width],
        after(down_col, up_high),
    )

    d_gate_late, d_up_late = after(d_gate, up_high), after(d_up, up_high)

    def normed_gradient(rows):
        return dot_nt(d_gate_late[rows], gate_all) + dot_nt(d_up_late[rows], up_all)

    d_normed_send = normed_gradient(slice(home, None)).astype(BF16)
    d_normed_got = to_half(d_normed_send)
    gate_sum = finish(
        dot_tn(after(low, d_normed_send), gate_mine), gate_core[:half_width], after(gate_col, d_normed_send)
    )
    d_normed = normed_gradient(slice(None, home)) + after(d_normed_got, gate_sum).astype(F32)

    gain_two_sum = jnp.sum(d_normed * hat_two, axis=0)
    d_hat = d_normed * gain_two
    mean_two = jnp.mean(d_hat * hat_two, axis=1, keepdims=True)
    d_resid = (cotangent[:home].astype(F32) + scale_two * (d_hat - hat_two * mean_two)).astype(BF16)
    d_resid_span = in_order(part_low, d_resid, to_half(d_resid), 0)

    activated_late, output_late = after(activated, d_resid), after(output_got, d_resid)
    output_own = dot(activated_late[:home], down_mine) + cols_of(resid_mid, slot, half_width)
    output_own = (output_own + output_late[home:].astype(F32)).astype(BF16)
    output_other = dot(activated_late[home:], down_mine) + after(resid_got, d_resid).astype(F32)
    output_other = (output_other + output_late[:home].astype(F32)).astype(BF16)
    output_half = in_order(part_low, output_own, output_other, 0)
    up_sum = finish(dot_tn(after(low, output_other), up_mine), up_core[:half_width], after(up_col, output_other))

    d_gated = dot_nt(d_resid_span, mixer_out)
    d_cproj = (d_gated * conved).astype(BF16)
    d_conved = d_gated * c_proj
    first_term = mask_one * d_conved
    second = mask_two * d_conved
    edge = to_core(jnp.concatenate([first_term[:edge_rows], second[:edge_rows]], axis=0))
    edge = jnp.where(core_low, swap_halves(edge, 1), 0.0)
    from_behind = kernel[1] * pad_rows(edge[:1], edge_rows - 1, 0) + kernel[2] * pad_rows(
        edge[edge_rows : edge_rows + 2], edge_rows - 2, 0
    )
    d_mixed = (
        kernel[0] * d_conved
        + kernel[1] * pad_rows(first_term[1:], 0, 1)
        + kernel[2] * pad_rows(second[2:], 0, 2)
        + pad_rows(from_behind, rest, 0)
    )
    kernel_sum = jnp.stack(
        [
            jnp.sum(d_conved * mixed_in, axis=0),
            jnp.sum(first_term * lag_one, axis=0) + jnp.sum(first_term[:edge_rows] * before_one, axis=0),
            jnp.sum(second * lag_two, axis=0) + jnp.sum(second[:edge_rows] * before_two, axis=0),
        ]
    )
    d_bproj = (d_mixed * x_proj).astype(BF16)
    d_xproj = (d_mixed * b_proj).astype(BF16)
    d_projected = jnp.stack([d_bproj, d_cproj, d_xproj])

    gated_late = after(gated_out, d_resid_span)
    out_core = to_core(dot_tn(gated_late[:, channels:], d_resid_span).astype(BF16))
    gated_mine = gated_late[:, :channels]
    out_high = dot_tn(gated_mine, d_resid_span[:, half_width:])
    out_high = (out_high + out_core[:, half_width:].astype(F32)).astype(BF16)
    out_col = to_col(out_high)

    def in_piece(left, pieces):
        return jnp.einsum("td,jtc->jdc", left, pieces, preferred_element_type=F32)

    in_core = to_core(in_piece(normed_one, d_projected[:, :, channels:]).astype(BF16))
    mine = d_projected[:, :, :channels]
    in_high = in_piece(normed_one[:, half_width:], mine)
    in_high = (in_high + in_core[:, half_width:].astype(F32)).astype(BF16)
    in_col = to_col(in_high)

    mixer_in_late = after(mixer_in, d_resid)

    def input_gradient(values, index):
        weights = lax.dynamic_slice_in_dim(mixer_in_late, index * half_width, half_width, axis=1)
        return jnp.einsum("jtc,jdc->td", values, weights, preferred_element_type=F32)

    d_projected_late = after(d_projected, in_high)
    one_send = input_gradient(d_projected_late, 1 - slot).astype(BF16)
    one_got = to_half(one_send)
    out_sum = finish(
        dot_tn(gated_mine, after(d_resid_span, one_send)[:, :half_width]),
        out_core[:, :half_width],
        out_col,
    )
    in_low = in_piece(after(normed_one[:, :half_width], one_send), mine)
    in_low = in_low + in_core[:, :half_width].astype(F32)
    d_normed_one = input_gradient(d_projected_late, slot) + one_got.astype(F32)

    block_output = scatter_span(after(output_half, one_send))

    hat_one = input_half.astype(F32) * scale_one
    gain_half = lax.dynamic_slice_in_dim(mixer_norm_gain, part * half_width, half_width)
    gain_one_sum = jnp.sum(d_normed_one * hat_one, axis=0)
    d_hat_one = d_normed_one * gain_half
    stat = jnp.sum(d_hat_one * hat_one, axis=1)
    mean_one = ((stat + to_half(stat)) / width)[:, None]
    d_input = cols_of(d_resid_span, slot, half_width).astype(F32) + scale_one * (d_hat_one - hat_one * mean_one)
    block_input_gradient = scatter_span(d_input)

    grad_down, _, _ = line_sum(down_sum, BF16, (d_resid,), (in_high,))
    grad_gate, _, _ = line_sum(gate_sum, BF16, (d_resid_span,), (d_normed_one,))
    grad_up, _, up_whole = line_sum(up_sum, BF16, (one_send,), (d_input,))
    grad_out, out_half, out_whole = line_sum(out_sum, BF16, (d_input,), (up_whole,))
    in_sum = in_low + in_col.astype(F32)
    grad_in, in_half, in_whole = line_sum(in_sum, BF16, (d_input, out_half), (out_whole,))

    kernel_sum = jnp.where(core_low, kernel_sum, swap_halves(kernel_sum, 1))
    halves = jnp.concatenate([kernel_sum, gain_one_sum[None]], axis=0)
    wide = in_order(part_low, halves, jnp.zeros_like(halves), 1)
    two = gain_two_sum[None]
    small = jnp.concatenate([wide, jnp.where(col_low, two, swap_halves(two, 1))], axis=0)
    small = small + to_core(small)
    small = small + to_col(small)
    small = small + to_half(small)
    small = line_sum(small, F32, (in_half,), (in_whole,))[0]
    small = lax.dynamic_slice_in_dim(small, (row * 2 + col) * own_width, own_width, axis=1)

    return (
        block_output,
        block_input_gradient,
        grad_in,
        grad_out,
        grad_gate,
        grad_up,
        grad_down,
        small[:3],
        small[3],
        small[4],
    )


def solution(mesh):
    placed = (
        P("dp", None, ("row", "col")),
        P("dp", None),
        P("dp", None, ("row", "col")),
        P(None, "col", "row"),
        P("row", "col"),
        P("col", "row"),
        P("col", "row"),
        P("row", "col"),
        P(None, ("row", "col")),
        P(),
        P(),
    )
    return jax.shard_map(
        body,
        mesh=mesh,
        in_specs=placed,
        out_specs=(
            P("dp", None, ("row", "col")),
            P("dp", None, ("row", "col")),
            P(None, "col", "row"),
            P("row", "col"),
            P("col", "row"),
            P("col", "row"),
            P("row", "col"),
            P(None, ("row", "col")),
            P(("row", "col")),
            P(("row", "col")),
        ),
        check_vma=False,
    )
```

profile of v0, /device:TPU:0, one launch (start us, length us, event | category | flops | bytes accessed | tf_op | source)
XLA Modules:
  0.0 514.3 jit_solution(13720035875891694158)
XLA Ops:
  5.4 11.0 %collective-permute-done = bf16[1792,128]{1,0:T(8,128)(2,1)S(1)} collective-permute-done((bf16[1792,128]{1,0:T(8,128)(2,1)S(1)}, bf16[1792,128]{1,0:T(8,128)(2,1)S(1)}, u32[]{:S(2)}, u32[]{:S(2)}) %collective-permute-start) | collective-permute-done | bytes 458784 | tf_op jit(solution)/shard_map/ppermute | solution.py:65
  24.7 8.5 %collective-permute-done.3 = bf16[3,512,256]{1,2,0:T(8,128)(2,1)S(1)} collective-permute-done((bf16[3,512,256]{1,2,0:T(8,128)(2,1)S(1)}, bf16[3,512,256]{1,2,0:T(8,128)(2,1)S(1)}, u32[]{:S(2)}, u32[]{:S(2)}) %collective-permute-start.3) | collective-permute-done | bytes 786464 | tf_op jit(solution)/shard_map/ppermute | solution.py:65
  44.7 4.5 convolution_bitcast_fusion
  59.3 4.1 collective-permute-done.12
  68.0 11.5 %collective-permute-done.10 = bf16[448,1024]{1,0:T(8,128)(2,1)} collective-permute-done((bf16[448,1024]{1,0:T(8,128)(2,1)}, bf16[448,1024]{1,0:T(8,128)(2,1)}, u32[]{:S(2)}, u32[]{:S(2)}) %collective-permute-start.10) | collective-permute-done | bytes 917536 | tf_op jit(solution)/shard_map/ppermute | solution.py:75
  85.0 18.3 %collective-permute-done.11 = bf16[448,1024]{1,0:T(8,128)(2,1)S(1)} collective-permute-done((bf16[448,1024]{1,0:T(8,128)(2,1)S(1)}, bf16[448,1024]{1,0:T(8,128)(2,1)S(1)}, u32[]{:S(2)}, u32[]{:S(2)}) %collective-permute-start.11) | collective-permute-done | bytes 917536 | tf_op jit(solution)/shard_map/ppermute | solution.py:75
  103.3 6.7 %fusion.63 = f32[896,2304]{1,0:T(8,128)} fusion(bf16[1024,1152]{1,0:T(8,128)(2,1)S(1)} %collective-permute-done.13, bf16[1024,1152]{1,0:T(8,128)(2,1)S(1)} %copy-done.41, bf16[448,1024]{1,0:T(8,128)(2,1)S(1)} %collective-permute-done.11, bf16[448,1024]{1,0:T(8,128)(2,1)S(1)} %multiply_convert_fusion.7), kind=kOutput, calls=%fused_computation.133 | convolution fusion | flops 4240965632 | bytes 14811136 | tf_op jit(solution)/shard_map/dot_general | solution.py:13
  113.0 11.0 %collective-permute-done.16 = bf16[1792,128]{1,0:T(8,128)(2,1)S(1)} collective-permute-done((bf16[1792,128]{1,0:T(8,128)(2,1)S(1)}, bf16[1792,128]{1,0:T(8,128)(2,1)S(1)}, u32[]{:S(2)}, u32[]{:S(2)}) %collective-permute-start.16) | collective-permute-done | bytes 458784 | tf_op jit(solution)/shard_map/ppermute | solution.py:65
  128.4 10.8 %multiply_convert_fusion.2 = (bf16[896,2304]{1,0:T(8,128)(2,1)S(1)}, f32[896,2304]{1,0:T(8,128)}) fusion(f32[896,2304]{1,0:T(8,128)} %fusion.63, bf16[1024,1152]{1,0:T(8,128)(2,1)S(1)} %collective-permute-done.15, bf16[1024,1152]{1,0:T(8,128)(2,1)S(1)} %constant_dynamic-update-slice_fusion.4, bf16[448,1024]{1,0:T(8,128)(2,1)S(1)} %collective-permute-done.11, ...), kind=kOutput, calls=%fused_computation.2 | convolution fusion | flops 4253351936 | bytes 27197440 | tf_op jit(solution)/shard_map/dot_general | solution.py:13
  139.2 9.8 %collective-permute-done.18 = bf16[896,512]{1,0:T(8,128)(2,1)S(1)} collective-permute-done((bf16[896,512]{1,0:T(8,128)(2,1)S(1)}, bf16[896,512]{1,0:T(8,128)(2,1)S(1)}, u32[]{:S(2)}, u32[]{:S(2)}) %collective-permute-start.18) | collective-permute-done | bytes 917536 | tf_op jit(solution)/shard_map/ppermute | solution.py:75
  149.3 3.9 convolution_convert_fusion.2
  158.2 5.2 %add_convert_fusion = bf16[1152,512]{1,0:T(8,128)(2,1)} fusion(bf16[1152,1024]{1,0:T(8,128)(2,1)} %collective-permute-done.19, bf16[448,1024]{1,0:T(8,128)(2,1)S(1)} %get-tuple-element.151, bf16[896,2304]{1,0:T(8,128)(2,1)} %copy-done.82, bf16[448,1024]{1,0:T(8,128)(2,1)S(1)} %copy-done.16), kind=kOutput, calls=%fused_computation.39 | convolution fusion | flops 1060569088 | bytes 6258688 | tf_op jit(solution)/shard_map/dot_general | solution.py:13
  163.4 4.8 fusion.56
  168.2 13.2 %multiply_convert_fusion.1 = (bf16[896,2304]{1,0:T(8,128)(2,1)S(1)}, bf16[896,2304]{1,0:T(8,128)(2,1)}) fusion(f32[896,2304]{1,0:T(8,128)} %fusion.63, f32[896,2304]{1,0:T(8,128)} %get-tuple-element.189, bf16[896,1024]{1,0:T(8,128)(2,1)S(1)} %pad_maximum_fusion.7, bf16[1152,1024]{1,0:T(8,128)(2,1)} %collective-permute-done.21, ...), kind=kOutput, calls=%fused_computation.1 | convolution fusion | flops 4264132608 | bytes 31326208 | tf_op jit(solution)/shard_map/dot_general | solution.py:13
  181.4 7.2 %convolution_convert_fusion.1 = bf16[1024,1152]{1,0:T(8,128)(2,1)} fusion(bf16[896,2304]{1,0:T(8,128)(2,1)} %get-tuple-element.53, bf16[448,1024]{1,0:T(8,128)(2,1)S(1)} %copy-done.38, bf16[448,1024]{1,0:T(8,128)(2,1)S(1)} %copy-done.18), kind=kOutput, calls=%fused_computation.13 | convolution fusion | flops 2118778880 | bytes 6258688 | tf_op jit(solution)/shard_map/dot_general | solution.py:13
  188.7 4.2 convolution_convert_fusion
  210.6 4.0 fusion.14
  214.7 3.9 add_convert_fusion.2
  218.7 11.5 %collective-permute-done.53 = bf16[1152,512]{1,0:T(8,128)(2,1)S(1)} collective-permute-done((bf16[1152,512]{1,0:T(8,128)(2,1)S(1)}, bf16[1152,512]{1,0:T(8,128)(2,1)S(1)}, u32[]{:S(2)}, u32[]{:S(2)}) %collective-permute-start.53) | collective-permute-done | bytes 1179680 | tf_op jit(solution)/shard_map/ppermute | solution.py:65
  238.5 3.9 fusion.20
  245.6 33.9 %collective-permute-done.25 = bf16[512,1152]{1,0:T(8,128)(2,1)S(1)} collective-permute-done((bf16[512,1152]{1,0:T(8,128)(2,1)S(1)}, bf16[512,1152]{1,0:T(8,128)(2,1)S(1)}, u32[]{:S(2)}, u32[]{:S(2)}) %collective-permute-start.25) | collective-permute-done | bytes 1179680 | tf_op jit(solution)/shard_map/ppermute | solution.py:65
  292.6 4.0 reduce-precision_convert_fusion.5
  297.9 11.7 %collective-permute-done.54 = bf16[1152,512]{1,0:T(8,128)(2,1)S(1)} collective-permute-done((bf16[1152,512]{1,0:T(8,128)(2,1)S(1)}, bf16[1152,512]{1,0:T(8,128)(2,1)S(1)}, u32[]{:S(2)}, u32[]{:S(2)}) %collective-permute-start.54) | collective-permute-done | bytes 1179680 | tf_op jit(solution)/shard_map/ppermute | solution.py:86
  312.6 7.5 %collective-permute-start.49 = (bf16[512,1152]{1,0:T(8,128)(2,1)}, bf16[512,1152]{1,0:T(8,128)(2,1)S(1)}, u32[]{:S(2)}, u32[]{:S(2)}) collective-permute-start(bf16[512,1152]{1,0:T(8,128)(2,1)} %get-tuple-element.132), channel_id=1, source_target_pairs={{0,8},{24,16},{1,9},{25,17},{2,10},{26,18},{3,11},{27,19},{4,12},{... | collective-permute-start | bytes 3538952 | tf_op jit(solution)/shard_map/ppermute | solution.py:86
  334.8 23.5 %collective-permute-done.49 = bf16[512,1152]{1,0:T(8,128)(2,1)S(1)} collective-permute-done((bf16[512,1152]{1,0:T(8,128)(2,1)}, bf16[512,1152]{1,0:T(8,128)(2,1)S(1)}, u32[]{:S(2)}, u32[]{:S(2)}) %collective-permute-start.49) | collective-permute-done | bytes 1179680 | tf_op jit(solution)/shard_map/ppermute | solution.py:86
  368.7 7.2 %collective-permute-start.41 = (bf16[256,512]{1,0:T(8,128)(2,1)S(1)}, bf16[256,512]{1,0:T(8,128)(2,1)S(1)}, u32[]{:S(2)}, u32[]{:S(2)}) collective-permute-start(bf16[256,512]{1,0:T(8,128)(2,1)S(1)} %get-tuple-element.193), channel_id=1, source_target_pairs={{0,8},{24,16},{1,9},{25,17},{2,10},{26,18},{3,11},{27,19},{4,12},{... | collective-permute-start | bytes 786440 | tf_op jit(solution)/shard_map/ppermute | solution.py:86
  386.3 6.7 %collective-permute-done.32 = bf16[1792,128]{1,0:T(8,128)(2,1)S(1)} collective-permute-done((bf16[1792,128]{1,0:T(8,128)(2,1)S(1)}, bf16[1792,128]{1,0:T(8,128)(2,1)S(1)}, u32[]{:S(2)}, u32[]{:S(2)}) %collective-permute-start.32) | collective-permute-done | bytes 458784 | tf_op jit(solution)/shard_map/ppermute | solution.py:65
  395.3 7.2 %collective-permute-start.38 = (bf16[3,512,256]{1,2,0:T(8,128)(2,1)S(1)}, bf16[3,512,256]{1,2,0:T(8,128)(2,1)S(1)}, u32[]{:S(2)}, u32[]{:S(2)}) collective-permute-start(bf16[3,512,256]{1,2,0:T(8,128)(2,1)S(1)} %get-tuple-element.191), channel_id=1, source_target_pairs={{0,8},{24,16},{1,9},{25,17},{2,10},{26,18},{3,11},{27,19},{4,12},{... | collective-permute-start | bytes 2359304 | tf_op jit(solution)/shard_map/ppermute | solution.py:86
  420.8 5.3 %collective-permute-done.56 = bf16[1152,512]{1,0:T(8,128)(2,1)S(1)} collective-permute-done((bf16[1152,512]{1,0:T(8,128)(2,1)S(1)}, bf16[1152,512]{1,0:T(8,128)(2,1)S(1)}, u32[]{:S(2)}, u32[]{:S(2)}) %collective-permute-start.56) | collective-permute-done | bytes 1179680 | tf_op jit(solution)/shard_map/ppermute | solution.py:95
  432.2 45.4 %collective-permute-done.48 = bf16[256,512]{1,0:T(8,128)(2,1)S(1)} collective-permute-done((bf16[256,512]{1,0:T(8,128)(2,1)S(1)}, bf16[256,512]{1,0:T(8,128)(2,1)S(1)}, u32[]{:S(2)}, u32[]{:S(2)}) %collective-permute-start.48) | collective-permute-done | bytes 262176 | tf_op jit(solution)/shard_map/ppermute | solution.py:95
  482.0 4.2 collective-permute-done.36
  494.0 17.3 %collective-permute-done.62 = f32[5,1024]{1,0:T(8,128)S(1)} collective-permute-done((f32[5,1024]{1,0:T(8,128)S(1)}, f32[5,1024]{1,0:T(8,128)S(1)}, u32[]{:S(2)}, u32[]{:S(2)}) %collective-permute-start.62) | collective-permute-done | bytes 20512 | tf_op jit(solution)/shard_map/ppermute | solution.py:95
  (423 shorter events, 179.6 us)
Async XLA Ops:
  5.3 27.9 %collective-permute-start.3 = (bf16[3,512,256]{1,2,0:T(8,128)(2,1)S(1)}, bf16[3,512,256]{1,2,0:T(8,128)(2,1)S(1)}, u32[]{:S(2)}, u32[]{:S(2)}) collective-permute-start(bf16[3,512,256]{1,2,0:T(8,128)(2,1)S(1)} %copy.58), channel_id=1, source_target_pairs={{0,1},{1,0},{2,3},{3,2},{4,5},{5,4},{6,7},{7,6},{8,9},{9,8},{10,11... | collective-permute-start | bytes 2359304 | tf_op jit(solution)/shard_map/ppermute | solution.py:65
  18.9 22.9 %collective-permute-start.2 = (bf16[896,512]{1,0:T(8,128)(2,1)S(1)}, bf16[896,512]{1,0:T(8,128)(2,1)}, u32[]{:S(2)}, u32[]{:S(2)}) collective-permute-start(bf16[896,512]{1,0:T(8,128)(2,1)S(1)} %maximum_select_fusion.4), channel_id=1, source_target_pairs={{0,4},{2,6},{4,0},{6,2},{1,5},{3,7},{5,1},{7,3},{8,12},{10,14},{12... | collective-permute-start | bytes 2752520 | tf_op jit(solution)/shard_map/ppermute | solution.py:75
  22.5 27.3 %collective-permute-start.8 = (bf16[256,512]{1,0:T(8,128)(2,1)}, bf16[256,512]{1,0:T(8,128)(2,1)}, u32[]{:S(2)}, u32[]{:S(2)}) collective-permute-start(bf16[256,512]{1,0:T(8,128)(2,1)} %param.15), channel_id=1, source_target_pairs={{0,1},{1,0},{2,3},{3,2},{4,5},{5,4},{6,7},{7,6},{8,9},{9,8},{10,11... | collective-permute-start | bytes 786440 | tf_op jit(solution)/shard_map/ppermute | solution.py:65
  23.1 40.3 %collective-permute-start.12 = (bf16[512,1152]{1,0:T(8,128)(2,1)}, bf16[512,1152]{1,0:T(8,128)(2,1)}, u32[]{:S(2)}, u32[]{:S(2)}) collective-permute-start(bf16[512,1152]{1,0:T(8,128)(2,1)} %param.16), channel_id=1, source_target_pairs={{0,1},{1,0},{2,3},{3,2},{4,5},{5,4},{6,7},{7,6},{8,9},{9,8},{10,11... | collective-permute-start | bytes 3538952 | tf_op jit(solution)/shard_map/ppermute | solution.py:65
  56.4 23.0 %collective-permute-start.10 = (bf16[448,1024]{1,0:T(8,128)(2,1)}, bf16[448,1024]{1,0:T(8,128)(2,1)}, u32[]{:S(2)}, u32[]{:S(2)}) collective-permute-start(bf16[448,1024]{1,0:T(8,128)(2,1)} %convolution_convert_fusion.3), channel_id=1, source_target_pairs={{0,4},{2,6},{4,0},{6,2},{1,5},{3,7},{5,1},{7,3},{8,12},{10,14},{12... | collective-permute-start | bytes 2752520 | tf_op jit(solution)/shard_map/ppermute | solution.py:75
  65.8 37.5 %collective-permute-start.13 = (bf16[1024,1152]{1,0:T(8,128)(2,1)}, bf16[1024,1152]{1,0:T(8,128)(2,1)S(1)}, u32[]{:S(2)}, u32[]{:S(2)}) collective-permute-start(bf16[1024,1152]{1,0:T(8,128)(2,1)} %constant_dynamic-update-slice_fusion.2), channel_id=1, source_target_pairs={{0,2},{2,0},{4,6},{6,4},{1,3},{3,1},{5,7},{7,5},{8,10},{10,8},{12,... | collective-permute-start | bytes 7077896 | tf_op jit(solution)/shard_map/ppermute | solution.py:70
  83.2 27.5 %collective-permute-start.14 = (bf16[512,1152]{1,0:T(8,128)(2,1)S(1)}, bf16[512,1152]{1,0:T(8,128)(2,1)S(1)}, u32[]{:S(2)}, u32[]{:S(2)}) collective-permute-start(bf16[512,1152]{1,0:T(8,128)(2,1)S(1)} %copy-done.34), channel_id=1, source_target_pairs={{0,1},{1,0},{2,3},{3,2},{4,5},{5,4},{6,7},{7,6},{8,9},{9,8},{10,11... | collective-permute-start | bytes 3538952 | tf_op jit(solution)/shard_map/ppermute | solution.py:65
  124.5 29.8 %collective-permute-start.20 = (bf16[1152,512]{1,0:T(8,128)(2,1)S(1)}, bf16[1152,512]{1,0:T(8,128)(2,1)S(1)}, u32[]{:S(2)}, u32[]{:S(2)}) collective-permute-start(bf16[1152,512]{1,0:T(8,128)(2,1)S(1)} %copy-done.35), channel_id=1, source_target_pairs={{0,1},{1,0},{2,3},{3,2},{4,5},{5,4},{6,7},{7,6},{8,9},{9,8},{10,11... | collective-permute-start | bytes 3538952 | tf_op jit(solution)/shard_map/ppermute | solution.py:65
  198.3 90.0 %collective-permute-start.27 = (bf16[448,512]{1,0:T(8,128)(2,1)S(1)}, bf16[448,512]{1,0:T(8,128)(2,1)S(1)}, u32[]{:S(2)}, u32[]{:S(2)}) collective-permute-start(bf16[448,512]{1,0:T(8,128)(2,1)S(1)} %dynamic-slice_convert_fusion.2), channel_id=1, source_target_pairs={{0,4},{2,6},{4,0},{6,2},{1,5},{3,7},{5,1},{7,3},{8,12},{10,14},{12... | collective-permute-start | bytes 1376264 | tf_op jit(solution)/shard_map/ppermute | solution.py:75
  200.2 88.1 %collective-permute-start.26 = (bf16[896,512]{1,0:T(8,128)(2,1)S(1)}, bf16[896,512]{1,0:T(8,128)(2,1)S(1)}, u32[]{:S(2)}, u32[]{:S(2)}) collective-permute-start(bf16[896,512]{1,0:T(8,128)(2,1)S(1)} %copy-done.75), channel_id=1, source_target_pairs={{0,4},{2,6},{4,0},{6,2},{1,5},{3,7},{5,1},{7,3},{8,12},{10,14},{12... | collective-permute-start | bytes 2752520 | tf_op jit(solution)/shard_map/ppermute | solution.py:75
  201.3 28.8 %collective-permute-start.53 = (bf16[1152,512]{1,0:T(8,128)(2,1)S(1)}, bf16[1152,512]{1,0:T(8,128)(2,1)S(1)}, u32[]{:S(2)}, u32[]{:S(2)}) collective-permute-start(bf16[1152,512]{1,0:T(8,128)(2,1)S(1)} %copy-done.74), channel_id=1, source_target_pairs={{0,1},{1,0},{2,3},{3,2},{4,5},{5,4},{6,7},{7,6},{8,9},{9,8},{10,11... | collective-permute-start | bytes 3538952 | tf_op jit(solution)/shard_map/ppermute | solution.py:65
  205.6 86.9 %collective-permute-start.44 = (bf16[512,1152]{1,0:T(8,128)(2,1)S(1)}, bf16[512,1152]{1,0:T(8,128)(2,1)S(1)}, u32[]{:S(2)}, u32[]{:S(2)}) collective-permute-start(bf16[512,1152]{1,0:T(8,128)(2,1)S(1)} %fusion.1), channel_id=1, source_target_pairs={{0,1},{1,0},{2,3},{3,2},{4,5},{5,4},{6,7},{7,6},{8,9},{9,8},{10,11... | collective-permute-start | bytes 3538952 | tf_op jit(solution)/shard_map/ppermute | solution.py:65
  209.4 70.1 %collective-permute-start.25 = (bf16[512,1152]{1,0:T(8,128)(2,1)S(1)}, bf16[512,1152]{1,0:T(8,128)(2,1)S(1)}, u32[]{:S(2)}, u32[]{:S(2)}) collective-permute-start(bf16[512,1152]{1,0:T(8,128)(2,1)S(1)} %fusion.2), channel_id=1, source_target_pairs={{0,1},{1,0},{2,3},{3,2},{4,5},{5,4},{6,7},{7,6},{8,9},{9,8},{10,11... | collective-permute-start | bytes 3538952 | tf_op jit(solution)/shard_map/ppermute | solution.py:65
  230.1 56.0 %collective-permute-start.23 = (bf16[448,1024]{1,0:T(8,128)(2,1)S(1)}, bf16[448,1024]{1,0:T(8,128)(2,1)S(1)}, u32[]{:S(2)}, u32[]{:S(2)}) collective-permute-start(bf16[448,1024]{1,0:T(8,128)(2,1)S(1)} %add_convert_fusion.2), channel_id=1, source_target_pairs={{0,4},{2,6},{4,0},{6,2},{1,5},{3,7},{5,1},{7,3},{8,12},{10,14},{12... | collective-permute-start | bytes 2752520 | tf_op jit(solution)/shard_map/ppermute | solution.py:75
  279.5 30.2 %collective-permute-start.54 = (bf16[1152,512]{1,0:T(8,128)(2,1)S(1)}, bf16[1152,512]{1,0:T(8,128)(2,1)S(1)}, u32[]{:S(2)}, u32[]{:S(2)}) collective-permute-start(bf16[1152,512]{1,0:T(8,128)(2,1)S(1)} %get-tuple-element.197), channel_id=1, source_target_pairs={{0,8},{24,16},{1,9},{25,17},{2,10},{26,18},{3,11},{27,19},{4,12},{... | collective-permute-start | bytes 3538952 | tf_op jit(solution)/shard_map/ppermute | solution.py:86
  287.5 35.9 %collective-permute-start.28 = (bf16[448,1024]{1,0:T(8,128)(2,1)S(1)}, bf16[448,1024]{1,0:T(8,128)(2,1)S(1)}, u32[]{:S(2)}, u32[]{:S(2)}) collective-permute-start(bf16[448,1024]{1,0:T(8,128)(2,1)S(1)} %add_convert_fusion.1), channel_id=1, source_target_pairs={{0,4},{2,6},{4,0},{6,2},{1,5},{3,7},{5,1},{7,3},{8,12},{10,14},{12... | collective-permute-start | bytes 2752520 | tf_op jit(solution)/shard_map/ppermute | solution.py:75
  296.6 72.1 %collective-permute-start.45 = (bf16[512,1152]{1,0:T(8,128)(2,1)}, bf16[512,1152]{1,0:T(8,128)(2,1)S(1)}, u32[]{:S(2)}, u32[]{:S(2)}) collective-permute-start(bf16[512,1152]{1,0:T(8,128)(2,1)} %get-tuple-element.195), channel_id=1, source_target_pairs={{0,8},{24,16},{1,9},{25,17},{2,10},{26,18},{3,11},{27,19},{4,12},{... | collective-permute-start | bytes 3538952 | tf_op jit(solution)/shard_map/ppermute | solution.py:86
  311.8 64.2 %collective-permute-start.55 = (bf16[1152,512]{1,0:T(8,128)(2,1)S(1)}, bf16[1152,512]{1,0:T(8,128)(2,1)S(1)}, u32[]{:S(2)}, u32[]{:S(2)}) collective-permute-start(bf16[1152,512]{1,0:T(8,128)(2,1)S(1)} %fusion.51), channel_id=1, source_target_pairs={{8,16},{16,8},{9,17},{17,9},{10,18},{18,10},{11,19},{19,11},{12,20... | collective-permute-start | bytes 3538952 | tf_op jit(solution)/shard_map/ppermute | solution.py:90
  312.6 45.7 %collective-permute-start.49 = (bf16[512,1152]{1,0:T(8,128)(2,1)}, bf16[512,1152]{1,0:T(8,128)(2,1)S(1)}, u32[]{:S(2)}, u32[]{:S(2)}) collective-permute-start(bf16[512,1152]{1,0:T(8,128)(2,1)} %get-tuple-element.132), channel_id=1, source_target_pairs={{0,8},{24,16},{1,9},{25,17},{2,10},{26,18},{3,11},{27,19},{4,12},{... | collective-permute-start | bytes 3538952 | tf_op jit(solution)/shard_map/ppermute | solution.py:86
  333.4 28.0 %collective-permute-start.30 = (bf16[3,1024,256]{1,2,0:T(8,128)(2,1)S(1)}, bf16[3,1024,256]{1,2,0:T(8,128)(2,1)S(1)}, u32[]{:S(2)}, u32[]{:S(2)}) collective-permute-start(bf16[3,1024,256]{1,2,0:T(8,128)(2,1)S(1)} %fusion.46), channel_id=1, source_target_pairs={{0,2},{2,0},{4,6},{6,4},{1,3},{3,1},{5,7},{7,5},{8,10},{10,8},{12,... | collective-permute-start | bytes 4718600 | tf_op jit(solution)/shard_map/ppermute | solution.py:70
  334.3 25.0 %collective-permute-start.39 = (bf16[256,1024]{1,0:T(8,128)(2,1)S(1)}, bf16[256,1024]{1,0:T(8,128)(2,1)S(1)}, u32[]{:S(2)}, u32[]{:S(2)}) collective-permute-start(bf16[256,1024]{1,0:T(8,128)(2,1)S(1)} %convolution_convert_fusion.4), channel_id=1, source_target_pairs={{0,2},{2,0},{4,6},{6,4},{1,3},{3,1},{5,7},{7,5},{8,10},{10,8},{12,... | collective-permute-start | bytes 1572872 | tf_op jit(solution)/shard_map/ppermute | solution.py:70
  358.6 45.9 %collective-permute-start.50 = (bf16[512,1152]{1,0:T(8,128)(2,1)S(1)}, bf16[512,1152]{1,0:T(8,128)(2,1)S(1)}, u32[]{:S(2)}, u32[]{:S(2)}) collective-permute-start(bf16[512,1152]{1,0:T(8,128)(2,1)S(1)} %fusion.50), channel_id=1, source_target_pairs={{8,16},{16,8},{9,17},{17,9},{10,18},{18,10},{11,19},{19,11},{12,20... | collective-permute-start | bytes 3538952 | tf_op jit(solution)/shard_map/ppermute | solution.py:90
  364.0 31.3 %collective-permute-start.33 = (bf16[896,512]{1,0:T(8,128)(2,1)S(1)}, bf16[896,512]{1,0:T(8,128)(2,1)S(1)}, u32[]{:S(2)}, u32[]{:S(2)}) collective-permute-start(bf16[896,512]{1,0:T(8,128)(2,1)S(1)} %bitcast_convert_fusion), channel_id=1, source_target_pairs={{0,4},{2,6},{4,0},{6,2},{1,5},{3,7},{5,1},{7,3},{8,12},{10,14},{12... | collective-permute-start | bytes 2752520 | tf_op jit(solution)/shard_map/ppermute | solution.py:75
  368.7 39.9 %collective-permute-start.41 = (bf16[256,512]{1,0:T(8,128)(2,1)S(1)}, bf16[256,512]{1,0:T(8,128)(2,1)S(1)}, u32[]{:S(2)}, u32[]{:S(2)}) collective-permute-start(bf16[256,512]{1,0:T(8,128)(2,1)S(1)} %get-tuple-element.193), channel_id=1, source_target_pairs={{0,8},{24,16},{1,9},{25,17},{2,10},{26,18},{3,11},{27,19},{4,12},{... | collective-permute-start | bytes 786440 | tf_op jit(solution)/shard_map/ppermute | solution.py:86
  384.4 34.3 %collective-permute-start.46 = (bf16[512,1152]{1,0:T(8,128)(2,1)S(1)}, bf16[512,1152]{1,0:T(8,128)(2,1)S(1)}, u32[]{:S(2)}, u32[]{:S(2)}) collective-permute-start(bf16[512,1152]{1,0:T(8,128)(2,1)S(1)} %fusion.49), channel_id=1, source_target_pairs={{8,16},{16,8},{9,17},{17,9},{10,18},{18,10},{11,19},{19,11},{12,20... | collective-permute-start | bytes 3538952 | tf_op jit(solution)/shard_map/ppermute | solution.py:90
  392.9 33.2 %collective-permute-start.56 = (bf16[1152,512]{1,0:T(8,128)(2,1)S(1)}, bf16[1152,512]{1,0:T(8,128)(2,1)S(1)}, u32[]{:S(2)}, u32[]{:S(2)}) collective-permute-start(bf16[1152,512]{1,0:T(8,128)(2,1)S(1)} %reduce-precision_convert_fusion), channel_id=1, source_target_pairs={{8,0},{16,24},{9,1},{17,25},{10,2},{18,26},{11,3},{19,27},{12,4},{... | collective-permute-start | bytes 3538952 | tf_op jit(solution)/shard_map/ppermute | solution.py:95
  395.3 84.8 %collective-permute-start.38 = (bf16[3,512,256]{1,2,0:T(8,128)(2,1)S(1)}, bf16[3,512,256]{1,2,0:T(8,128)(2,1)S(1)}, u32[]{:S(2)}, u32[]{:S(2)}) collective-permute-start(bf16[3,512,256]{1,2,0:T(8,128)(2,1)S(1)} %get-tuple-element.191), channel_id=1, source_target_pairs={{0,8},{24,16},{1,9},{25,17},{2,10},{26,18},{3,11},{27,19},{4,12},{... | collective-permute-start | bytes 2359304 | tf_op jit(solution)/shard_map/ppermute | solution.py:86
  408.7 78.9 %collective-permute-start.51 = (bf16[512,1152]{1,0:T(8,128)(2,1)S(1)}, bf16[512,1152]{1,0:T(8,128)(2,1)S(1)}, u32[]{:S(2)}, u32[]{:S(2)}) collective-permute-start(bf16[512,1152]{1,0:T(8,128)(2,1)S(1)} %reduce-precision_convert_fusion.2), channel_id=1, source_target_pairs={{8,0},{16,24},{9,1},{17,25},{10,2},{18,26},{11,3},{19,27},{12,4},{... | collective-permute-start | bytes 3538952 | tf_op jit(solution)/shard_map/ppermute | solution.py:95
  426.1 55.1 %collective-permute-start.60 = (f32[5,1024]{1,0:T(8,128)S(1)}, f32[5,1024]{1,0:T(8,128)S(1)}, u32[]{:S(2)}, u32[]{:S(2)}) collective-permute-start(f32[5,1024]{1,0:T(8,128)S(1)} %add.381), channel_id=1, source_target_pairs={{0,8},{24,16},{1,9},{25,17},{2,10},{26,18},{3,11},{27,19},{4,12},{... | collective-permute-start | bytes 61448 | tf_op jit(solution)/shard_map/ppermute | solution.py:86
  429.1 63.3 %collective-permute-start.52 = (bf16[512,1152]{1,0:T(8,128)(2,1)S(1)}, bf16[512,1152]{1,0:T(8,128)(2,1)S(1)}, u32[]{:S(2)}, u32[]{:S(2)}) collective-permute-start(bf16[512,1152]{1,0:T(8,128)(2,1)S(1)} %reduce-precision_convert_fusion.4), channel_id=1, source_target_pairs={{8,0},{16,24},{9,1},{17,25},{10,2},{18,26},{11,3},{19,27},{12,4},{... | collective-permute-start | bytes 3538952 | tf_op jit(solution)/shard_map/ppermute | solution.py:95
  430.6 47.1 %collective-permute-start.48 = (bf16[256,512]{1,0:T(8,128)(2,1)S(1)}, bf16[256,512]{1,0:T(8,128)(2,1)S(1)}, u32[]{:S(2)}, u32[]{:S(2)}) collective-permute-start(bf16[256,512]{1,0:T(8,128)(2,1)S(1)} %reduce-precision_convert_fusion.8), channel_id=1, source_target_pairs={{8,0},{16,24},{9,1},{17,25},{10,2},{18,26},{11,3},{19,27},{12,4},{... | collective-permute-start | bytes 786440 | tf_op jit(solution)/shard_map/ppermute | solution.py:95
  489.8 22.6 %collective-permute-start.47 = (bf16[3,512,256]{1,2,0:T(8,128)(2,1)S(1)}, bf16[3,512,256]{1,2,0:T(8,128)(2,1)S(1)}, u32[]{:S(2)}, u32[]{:S(2)}) collective-permute-start(bf16[3,512,256]{1,2,0:T(8,128)(2,1)S(1)} %reduce-precision_convert_fusion.6), channel_id=1, source_target_pairs={{8,0},{16,24},{9,1},{17,25},{10,2},{18,26},{11,3},{19,27},{12,4},{... | collective-permute-start | bytes 2359304 | tf_op jit(solution)/shard_map/ppermute | solution.py:95
  (120 other events, 941.7 us)
where the time goes:
time: 521 us; the launch traced here: 514 us
  waiting for transfers between devices  256 us (49%)
  matrix products  112 us (21%)
  starting transfers between devices  79 us (15%)
  other arithmetic  43.1 us (8%)
  local copies, waits for them, and re-layouts  22 us (4%)
    dot_general x25, matrix products, contract(): lax.dot_general(left, right, (((left_axis,), (right_axis,)), ((), ())), p...  99.8 us
    ppermute x16, waiting for transfers between devices, to_col(): return lax.ppermute(values, 'col', [(i, size - 1 - i) for i in range(size)])  99.5 us
    ppermute x6, waiting for transfers between devices, line_sum(): got = lax.ppermute(result, 'dp', pairs)  68.1 us
    ppermute x11, waiting for transfers between devices, to_half(): lax.ppermute(values, 'row', [(i, (i + size // 2) % size) for i in range(s...  49 us
    ppermute x6, waiting for transfers between devices, line_sum(): lax.ppermute(keep(total).astype(dtype), 'dp', pairs)  35.2 us
    ppermute x6, starting transfers between devices, line_sum(): lax.ppermute(keep(total).astype(dtype), 'dp', pairs)  28.5 us
    ppermute x16, starting transfers between devices, to_col(): return lax.ppermute(values, 'col', [(i, size - 1 - i) for i in range(size)])  22 us
    ppermute x11, starting transfers between devices, to_half(): lax.ppermute(values, 'row', [(i, (i + size // 2) % size) for i in range(s...  13.6 us
  transfers between devices with their start and end apart: 63, of which 27 were waited for; matrix products, arithmetic and copies ran while one was open for 28% of the time, Pallas kernels for 0%

commit v1 on v0

--- a/solution.py
+++ b/solution.py
@@ -89,13 +89,17 @@
     pairs = [(middle - 1, middle), (middle, middle - 1)]
     got = after(lax.ppermute(half, "dp", pairs), *outward_after)
     whole = keep(keep(total) + got.astype(F32)).astype(dtype)
-    result = whole
-    for step in range(middle - 1):
-        pairs = [(middle - 1 - step, middle - 2 - step), (middle + step, middle + step + 1)]
-        got = lax.ppermute(result, "dp", pairs)
-        taker = (place == middle - 2 - step) | (place == middle + step + 1)
-        result = jnp.where(taker, got, result)
-    return result.astype(F32), half, whole
+
+    def outward(*end_after):
+        result = whole
+        for step in range(middle - 1):
+            pairs = [(middle - 1 - step, middle - 2 - step), (middle + step, middle + step + 1)]
+            got = after(lax.ppermute(result, "dp", pairs), *end_after)
+            taker = (place == middle - 2 - step) | (place == middle + step + 1)
+            result = jnp.where(taker, got, result)
+        return result.astype(F32)
+
+    return outward, half, whole
 
 
 def body(
@@ -364,12 +368,15 @@
     d_input = cols_of(d_resid_span, slot, half_width).astype(F32) + scale_one * (d_hat_one - hat_one * mean_one)
     block_input_gradient = scatter_span(d_input)
 
-    grad_down, _, _ = line_sum(down_sum, BF16, (d_resid,), (in_high,))
-    grad_gate, _, _ = line_sum(gate_sum, BF16, (d_resid_span,), (d_normed_one,))
-    grad_up, _, up_whole = line_sum(up_sum, BF16, (one_send,), (d_input,))
-    grad_out, out_half, out_whole = line_sum(out_sum, BF16, (d_input,), (up_whole,))
     in_sum = in_low + in_col.astype(F32)
-    grad_in, in_half, in_whole = line_sum(in_sum, BF16, (d_input, out_half), (out_whole,))
+    late = (d_input,)
+    up_out, up_half, up_whole = line_sum(up_sum, BF16, (one_send,), late)
+    out_out, out_half, out_whole = line_sum(out_sum, BF16, late, (up_whole,))
+    in_out, in_half, in_whole = line_sum(in_sum, BF16, (d_input, out_half), (out_whole,))
+    down_out, _, _ = line_sum(down_sum, BF16, (d_resid,), (d_cproj,))
+    gate_out, _, _ = line_sum(gate_sum, BF16, (d_resid_span,), (up_half,))
+    grad_down, grad_gate = down_out(d_input, out_half), gate_out(in_half)
+    grad_up, grad_out, grad_in = up_out(in_whole), out_out(in_whole), in_out()
 
     kernel_sum = jnp.where(core_low, kernel_sum, swap_halves(kernel_sum, 1))
     halves = jnp.concatenate([kernel_sum, gain_one_sum[None]], axis=0)
@@ -379,7 +386,7 @@
     small = small + to_core(small)
     small = small + to_col(small)
     small = small + to_half(small)
-    small = line_sum(small, F32, (in_half,), (in_whole,))[0]
+    small = line_sum(small, F32, (in_whole,))[0]()
     small = lax.dynamic_slice_in_dim(small, (row * 2 + col) * own_width, own_width, axis=1)
 
     return (

time: 521 us -> 495 us (0.950)
  waiting for transfers between devices: 256 us -> 222 us
  starting transfers between devices: 79 us -> 87.7 us
    ppermute x6, waiting for transfers between devices: 68.1 us -> 29.6 us  [outward(): got = after(lax.ppermute(result, 'dp', pairs), *end_after)]
    ppermute x6, starting transfers between devices: 28.5 us -> 36.5 us  [line_sum(): lax.ppermute(keep(total).astype(dtype), 'dp', pairs)]
    ppermute x16, waiting for transfers between devices: 99.5 us -> 105 us  [to_col(): return lax.ppermute(values, 'col', [(i, size - 1 - i) for i in range(size)])]
    unnamed x182 -> x176, local copies, waits for them, and re-layouts: 11.8 us -> 11.6 us
  transfers between devices with their start and end apart: 63 -> 63, of which waited for: 27 -> 25; matrix products, arithmetic and copies ran while one was open for 28% -> 29% of each run, Pallas kernels for 0% -> 0%
where the time goes in v1:
time: 495 us; the launch traced here: 489 us
  waiting for transfers between devices  222 us (45%)
  matrix products  112 us (23%)
  starting transfers between devices  87.7 us (18%)
  other arithmetic  42.5 us (9%)
  local copies, waits for them, and re-layouts  21.8 us (4%)
    ppermute x16, waiting for transfers between devices, to_col(): return lax.ppermute(values, 'col', [(i, size - 1 - i) for i in range(size)])  105 us
    dot_general x25, matrix products, contract(): lax.dot_general(left, right, (((left_axis,), (right_axis,)), ((), ())), p...  100 us
    ppermute x11, waiting for transfers between devices, to_half(): lax.ppermute(values, 'row', [(i, (i + size // 2) % size) for i in range(s...  50 us
    ppermute x6, starting transfers between devices, line_sum(): lax.ppermute(keep(total).astype(dtype), 'dp', pairs)  36.5 us
    ppermute x6, waiting for transfers between devices, line_sum(): lax.ppermute(keep(total).astype(dtype), 'dp', pairs)  32.6 us
    ppermute x6, waiting for transfers between devices, outward(): got = after(lax.ppermute(result, 'dp', pairs), *end_after)  29.6 us
    ppermute x16, starting transfers between devices, to_col(): return lax.ppermute(values, 'col', [(i, size - 1 - i) for i in range(size)])  22.1 us
    ppermute x11, starting transfers between devices, to_half(): lax.ppermute(values, 'row', [(i, (i + size // 2) % size) for i in range(s...  13.1 us
  transfers between devices with their start and end apart: 63, of which 25 were waited for; matrix products, arithmetic and copies ran while one was open for 29% of the time, Pallas kernels for 0%

profile of v1, /device:TPU:0, one launch (start us, length us, event | category | flops | bytes accessed | tf_op | source)
XLA Modules:
  0.0 489.0 jit_solution(14618500696029758966)
XLA Ops:
  5.4 11.0 %collective-permute-done = bf16[1792,128]{1,0:T(8,128)(2,1)S(1)} collective-permute-done((bf16[1792,128]{1,0:T(8,128)(2,1)S(1)}, bf16[1792,128]{1,0:T(8,128)(2,1)S(1)}, u32[]{:S(2)}, u32[]{:S(2)}) %collective-permute-start) | collective-permute-done | bytes 458784 | tf_op jit(solution)/shard_map/ppermute | solution.py:65
  24.7 8.5 %collective-permute-done.3 = bf16[3,512,256]{1,2,0:T(8,128)(2,1)S(1)} collective-permute-done((bf16[3,512,256]{1,2,0:T(8,128)(2,1)S(1)}, bf16[3,512,256]{1,2,0:T(8,128)(2,1)S(1)}, u32[]{:S(2)}, u32[]{:S(2)}) %collective-permute-start.3) | collective-permute-done | bytes 786464 | tf_op jit(solution)/shard_map/ppermute | solution.py:65
  44.7 4.5 convolution_bitcast_fusion
  59.3 4.1 collective-permute-done.12
  68.0 11.5 %collective-permute-done.10 = bf16[448,1024]{1,0:T(8,128)(2,1)} collective-permute-done((bf16[448,1024]{1,0:T(8,128)(2,1)}, bf16[448,1024]{1,0:T(8,128)(2,1)}, u32[]{:S(2)}, u32[]{:S(2)}) %collective-permute-start.10) | collective-permute-done | bytes 917536 | tf_op jit(solution)/shard_map/ppermute | solution.py:75
  85.0 18.3 %collective-permute-done.11 = bf16[448,1024]{1,0:T(8,128)(2,1)S(1)} collective-permute-done((bf16[448,1024]{1,0:T(8,128)(2,1)S(1)}, bf16[448,1024]{1,0:T(8,128)(2,1)S(1)}, u32[]{:S(2)}, u32[]{:S(2)}) %collective-permute-start.11) | collective-permute-done | bytes 917536 | tf_op jit(solution)/shard_map/ppermute | solution.py:75
  103.3 6.6 %fusion.63 = f32[896,2304]{1,0:T(8,128)} fusion(bf16[1024,1152]{1,0:T(8,128)(2,1)S(1)} %collective-permute-done.13, bf16[1024,1152]{1,0:T(8,128)(2,1)S(1)} %copy-done.41, bf16[448,1024]{1,0:T(8,128)(2,1)S(1)} %collective-permute-done.11, bf16[448,1024]{1,0:T(8,128)(2,1)S(1)} %multiply_convert_fusion.7), kind=kOutput, calls=%fused_computation.133 | convolution fusion | flops 4240965632 | bytes 14811136 | tf_op jit(solution)/shard_map/dot_general | solution.py:13
  113.0 11.1 %collective-permute-done.16 = bf16[1792,128]{1,0:T(8,128)(2,1)S(1)} collective-permute-done((bf16[1792,128]{1,0:T(8,128)(2,1)S(1)}, bf16[1792,128]{1,0:T(8,128)(2,1)S(1)}, u32[]{:S(2)}, u32[]{:S(2)}) %collective-permute-start.16) | collective-permute-done | bytes 458784 | tf_op jit(solution)/shard_map/ppermute | solution.py:65
  128.4 10.8 %multiply_convert_fusion.2 = (bf16[896,2304]{1,0:T(8,128)(2,1)S(1)}, f32[896,2304]{1,0:T(8,128)}) fusion(f32[896,2304]{1,0:T(8,128)} %fusion.63, bf16[1024,1152]{1,0:T(8,128)(2,1)S(1)} %collective-permute-done.15, bf16[1024,1152]{1,0:T(8,128)(2,1)S(1)} %constant_dynamic-update-slice_fusion.4, bf16[448,1024]{1,0:T(8,128)(2,1)S(1)} %collective-permute-done.11, ...), kind=kOutput, calls=%fused_computation.2 | convolution fusion | flops 4253351936 | bytes 27197440 | tf_op jit(solution)/shard_map/dot_general | solution.py:13
  139.2 9.8 %collective-permute-done.18 = bf16[896,512]{1,0:T(8,128)(2,1)S(1)} collective-permute-done((bf16[896,512]{1,0:T(8,128)(2,1)S(1)}, bf16[896,512]{1,0:T(8,128)(2,1)S(1)}, u32[]{:S(2)}, u32[]{:S(2)}) %collective-permute-start.18) | collective-permute-done | bytes 917536 | tf_op jit(solution)/shard_map/ppermute | solution.py:75
  149.3 3.9 convolution_convert_fusion.2
  158.2 5.2 %add_convert_fusion = bf16[1152,512]{1,0:T(8,128)(2,1)} fusion(bf16[1152,1024]{1,0:T(8,128)(2,1)} %collective-permute-done.19, bf16[448,1024]{1,0:T(8,128)(2,1)S(1)} %get-tuple-element.157, bf16[896,2304]{1,0:T(8,128)(2,1)} %copy-done.80, bf16[448,1024]{1,0:T(8,128)(2,1)S(1)} %copy-done.16), kind=kOutput, calls=%fused_computation.39 | convolution fusion | flops 1060569088 | bytes 6258688 | tf_op jit(solution)/shard_map/dot_general | solution.py:13
  163.4 4.8 fusion.56
  168.2 13.2 %multiply_convert_fusion.1 = (bf16[896,2304]{1,0:T(8,128)(2,1)S(1)}, bf16[896,2304]{1,0:T(8,128)(2,1)}) fusion(f32[896,2304]{1,0:T(8,128)} %fusion.63, f32[896,2304]{1,0:T(8,128)} %get-tuple-element.195, bf16[896,1024]{1,0:T(8,128)(2,1)S(1)} %pad_maximum_fusion.7, bf16[1152,1024]{1,0:T(8,128)(2,1)} %collective-permute-done.21, ...), kind=kOutput, calls=%fused_computation.1 | convolution fusion | flops 4264132608 | bytes 31326208 | tf_op jit(solution)/shard_map/dot_general | solution.py:13
  181.4 7.2 %convolution_convert_fusion.1 = bf16[1024,1152]{1,0:T(8,128)(2,1)} fusion(bf16[896,2304]{1,0:T(8,128)(2,1)} %get-tuple-element.56, bf16[448,1024]{1,0:T(8,128)(2,1)S(1)} %copy-done.38, bf16[448,1024]{1,0:T(8,128)(2,1)S(1)} %copy-done.18), kind=kOutput, calls=%fused_computation.13 | convolution fusion | flops 2118778880 | bytes 6258688 | tf_op jit(solution)/shard_map/dot_general | solution.py:13
  188.7 4.2 convolution_convert_fusion
  210.6 4.1 fusion.14
  214.7 3.9 add_convert_fusion.2
  218.7 11.5 %collective-permute-done.53 = bf16[1152,512]{1,0:T(8,128)(2,1)S(1)} collective-permute-done((bf16[1152,512]{1,0:T(8,128)(2,1)S(1)}, bf16[1152,512]{1,0:T(8,128)(2,1)S(1)}, u32[]{:S(2)}, u32[]{:S(2)}) %collective-permute-start.53) | collective-permute-done | bytes 1179680 | tf_op jit(solution)/shard_map/ppermute | solution.py:65
  245.6 34.0 %collective-permute-done.25 = bf16[512,1152]{1,0:T(8,128)(2,1)S(1)} collective-permute-done((bf16[512,1152]{1,0:T(8,128)(2,1)S(1)}, bf16[512,1152]{1,0:T(8,128)(2,1)S(1)}, u32[]{:S(2)}, u32[]{:S(2)}) %collective-permute-start.25) | collective-permute-done | bytes 1179680 | tf_op jit(solution)/shard_map/ppermute | solution.py:65
  287.3 4.0 fusion.76
  291.3 4.0 reduce-precision_convert_fusion.5
  296.7 13.0 %collective-permute-done.54 = bf16[1152,512]{1,0:T(8,128)(2,1)S(1)} collective-permute-done((bf16[1152,512]{1,0:T(8,128)(2,1)S(1)}, bf16[1152,512]{1,0:T(8,128)(2,1)S(1)}, u32[]{:S(2)}, u32[]{:S(2)}) %collective-permute-start.54) | collective-permute-done | bytes 1179680 | tf_op jit(solution)/shard_map/ppermute | solution.py:86
  313.5 6.6 %collective-permute-start.49 = (bf16[512,1152]{1,0:T(8,128)(2,1)S(1)}, bf16[512,1152]{1,0:T(8,128)(2,1)S(1)}, u32[]{:S(2)}, u32[]{:S(2)}) collective-permute-start(bf16[512,1152]{1,0:T(8,128)(2,1)S(1)} %get-tuple-element.138), channel_id=1, source_target_pairs={{0,8},{24,16},{1,9},{25,17},{2,10},{26,18},{3,11},{27,19},{4,12},{... | collective-permute-start | bytes 3538952 | tf_op jit(solution)/shard_map/ppermute | solution.py:86
  338.6 19.6 %collective-permute-done.49 = bf16[512,1152]{1,0:T(8,128)(2,1)S(1)} collective-permute-done((bf16[512,1152]{1,0:T(8,128)(2,1)S(1)}, bf16[512,1152]{1,0:T(8,128)(2,1)S(1)}, u32[]{:S(2)}, u32[]{:S(2)}) %collective-permute-start.49) | collective-permute-done | bytes 1179680 | tf_op jit(solution)/shard_map/ppermute | solution.py:86
  372.1 13.8 %collective-permute-done.37 = bf16[3,512,256]{1,2,0:T(8,128)(2,1)S(1)} collective-permute-done((bf16[3,512,256]{1,2,0:T(8,128)(2,1)S(1)}, bf16[3,512,256]{1,2,0:T(8,128)(2,1)S(1)}, u32[]{:S(2)}, u32[]{:S(2)}) %collective-permute-start.37) | collective-permute-done | bytes 786464 | tf_op jit(solution)/shard_map/ppermute | solution.py:65
  385.9 12.8 %collective-permute-start.41 = (bf16[256,512]{1,0:T(8,128)(2,1)S(1)}, bf16[256,512]{1,0:T(8,128)(2,1)S(1)}, u32[]{:S(2)}, u32[]{:S(2)}) collective-permute-start(bf16[256,512]{1,0:T(8,128)(2,1)S(1)} %get-tuple-element.199), channel_id=1, source_target_pairs={{0,8},{24,16},{1,9},{25,17},{2,10},{26,18},{3,11},{27,19},{4,12},{... | collective-permute-start | bytes 786440 | tf_op jit(solution)/shard_map/ppermute | solution.py:86
  407.8 9.1 %collective-permute-start.38 = (bf16[3,512,256]{1,2,0:T(8,128)(2,1)S(1)}, bf16[3,512,256]{1,2,0:T(8,128)(2,1)S(1)}, u32[]{:S(2)}, u32[]{:S(2)}) collective-permute-start(bf16[3,512,256]{1,2,0:T(8,128)(2,1)S(1)} %get-tuple-element.197), channel_id=1, source_target_pairs={{0,8},{24,16},{1,9},{25,17},{2,10},{26,18},{3,11},{27,19},{4,12},{... | collective-permute-start | bytes 2359304 | tf_op jit(solution)/shard_map/ppermute | solution.py:86
  440.3 8.3 %collective-permute-done.36 = bf16[1792,128]{1,0:T(8,128)(2,1)S(1)} collective-permute-done((bf16[1792,128]{1,0:T(8,128)(2,1)S(1)}, bf16[1792,128]{1,0:T(8,128)(2,1)S(1)}, u32[]{:S(2)}, u32[]{:S(2)}) %collective-permute-start.36) | collective-permute-done | bytes 458784 | tf_op jit(solution)/shard_map/ppermute | solution.py:65
  452.7 10.9 %collective-permute-done.52 = bf16[512,1152]{1,0:T(8,128)(2,1)S(1)} collective-permute-done((bf16[512,1152]{1,0:T(8,128)(2,1)S(1)}, bf16[512,1152]{1,0:T(8,128)(2,1)S(1)}, u32[]{:S(2)}, u32[]{:S(2)}) %collective-permute-start.52) | collective-permute-done | bytes 1179680 | tf_op jit(solution)/shard_map/ppermute | solution.py:97
  465.1 4.1 collective-permute-done.48
  471.3 14.7 %collective-permute-done.62 = f32[5,1024]{1,0:T(8,128)S(1)} collective-permute-done((f32[5,1024]{1,0:T(8,128)S(1)}, f32[5,1024]{1,0:T(8,128)S(1)}, u32[]{:S(2)}, u32[]{:S(2)}) %collective-permute-start.62) | collective-permute-done | bytes 20512 | tf_op jit(solution)/shard_map/ppermute | solution.py:97
  (417 shorter events, 177.4 us)
Async XLA Ops:
  5.3 27.9 %collective-permute-start.3 = (bf16[3,512,256]{1,2,0:T(8,128)(2,1)S(1)}, bf16[3,512,256]{1,2,0:T(8,128)(2,1)S(1)}, u32[]{:S(2)}, u32[]{:S(2)}) collective-permute-start(bf16[3,512,256]{1,2,0:T(8,128)(2,1)S(1)} %copy.58), channel_id=1, source_target_pairs={{0,1},{1,0},{2,3},{3,2},{4,5},{5,4},{6,7},{7,6},{8,9},{9,8},{10,11... | collective-permute-start | bytes 2359304 | tf_op jit(solution)/shard_map/ppermute | solution.py:65
  22.5 27.3 %collective-permute-start.8 = (bf16[256,512]{1,0:T(8,128)(2,1)}, bf16[256,512]{1,0:T(8,128)(2,1)}, u32[]{:S(2)}, u32[]{:S(2)}) collective-permute-start(bf16[256,512]{1,0:T(8,128)(2,1)} %param.15), channel_id=1, source_target_pairs={{0,1},{1,0},{2,3},{3,2},{4,5},{5,4},{6,7},{7,6},{8,9},{9,8},{10,11... | collective-permute-start | bytes 786440 | tf_op jit(solution)/shard_map/ppermute | solution.py:65
  23.1 40.3 %collective-permute-start.12 = (bf16[512,1152]{1,0:T(8,128)(2,1)}, bf16[512,1152]{1,0:T(8,128)(2,1)}, u32[]{:S(2)}, u32[]{:S(2)}) collective-permute-start(bf16[512,1152]{1,0:T(8,128)(2,1)} %param.16), channel_id=1, source_target_pairs={{0,1},{1,0},{2,3},{3,2},{4,5},{5,4},{6,7},{7,6},{8,9},{9,8},{10,11... | collective-permute-start | bytes 3538952 | tf_op jit(solution)/shard_map/ppermute | solution.py:65
  56.4 23.0 %collective-permute-start.10 = (bf16[448,1024]{1,0:T(8,128)(2,1)}, bf16[448,1024]{1,0:T(8,128)(2,1)}, u32[]{:S(2)}, u32[]{:S(2)}) collective-permute-start(bf16[448,1024]{1,0:T(8,128)(2,1)} %convolution_convert_fusion.3), channel_id=1, source_target_pairs={{0,4},{2,6},{4,0},{6,2},{1,5},{3,7},{5,1},{7,3},{8,12},{10,14},{12... | collective-permute-start | bytes 2752520 | tf_op jit(solution)/shard_map/ppermute | solution.py:75
  65.8 37.5 %collective-permute-start.13 = (bf16[1024,1152]{1,0:T(8,128)(2,1)}, bf16[1024,1152]{1,0:T(8,128)(2,1)S(1)}, u32[]{:S(2)}, u32[]{:S(2)}) collective-permute-start(bf16[1024,1152]{1,0:T(8,128)(2,1)} %constant_dynamic-update-slice_fusion.2), channel_id=1, source_target_pairs={{0,2},{2,0},{4,6},{6,4},{1,3},{3,1},{5,7},{7,5},{8,10},{10,8},{12,... | collective-permute-start | bytes 7077896 | tf_op jit(solution)/shard_map/ppermute | solution.py:70
  83.2 27.5 %collective-permute-start.14 = (bf16[512,1152]{1,0:T(8,128)(2,1)S(1)}, bf16[512,1152]{1,0:T(8,128)(2,1)S(1)}, u32[]{:S(2)}, u32[]{:S(2)}) collective-permute-start(bf16[512,1152]{1,0:T(8,128)(2,1)S(1)} %copy-done.34), channel_id=1, source_target_pairs={{0,1},{1,0},{2,3},{3,2},{4,5},{5,4},{6,7},{7,6},{8,9},{9,8},{10,11... | collective-permute-start | bytes 3538952 | tf_op jit(solution)/shard_map/ppermute | solution.py:65
  124.5 29.8 %collective-permute-start.20 = (bf16[1152,512]{1,0:T(8,128)(2,1)S(1)}, bf16[1152,512]{1,0:T(8,128)(2,1)S(1)}, u32[]{:S(2)}, u32[]{:S(2)}) collective-permute-start(bf16[1152,512]{1,0:T(8,128)(2,1)S(1)} %copy-done.35), channel_id=1, source_target_pairs={{0,1},{1,0},{2,3},{3,2},{4,5},{5,4},{6,7},{7,6},{8,9},{9,8},{10,11... | collective-permute-start | bytes 3538952 | tf_op jit(solution)/shard_map/ppermute | solution.py:65
  198.3 89.0 %collective-permute-start.27 = (bf16[448,512]{1,0:T(8,128)(2,1)S(1)}, bf16[448,512]{1,0:T(8,128)(2,1)}, u32[]{:S(2)}, u32[]{:S(2)}) collective-permute-start(bf16[448,512]{1,0:T(8,128)(2,1)S(1)} %dynamic-slice_convert_fusion.2), channel_id=1, source_target_pairs={{0,4},{2,6},{4,0},{6,2},{1,5},{3,7},{5,1},{7,3},{8,12},{10,14},{12... | collective-permute-start | bytes 1376264 | tf_op jit(solution)/shard_map/ppermute | solution.py:75
  200.2 87.1 %collective-permute-start.26 = (bf16[896,512]{1,0:T(8,128)(2,1)S(1)}, bf16[896,512]{1,0:T(8,128)(2,1)S(1)}, u32[]{:S(2)}, u32[]{:S(2)}) collective-permute-start(bf16[896,512]{1,0:T(8,128)(2,1)S(1)} %copy-done.75), channel_id=1, source_target_pairs={{0,4},{2,6},{4,0},{6,2},{1,5},{3,7},{5,1},{7,3},{8,12},{10,14},{12... | collective-permute-start | bytes 2752520 | tf_op jit(solution)/shard_map/ppermute | solution.py:75
  201.3 28.8 %collective-permute-start.53 = (bf16[1152,512]{1,0:T(8,128)(2,1)S(1)}, bf16[1152,512]{1,0:T(8,128)(2,1)S(1)}, u32[]{:S(2)}, u32[]{:S(2)}) collective-permute-start(bf16[1152,512]{1,0:T(8,128)(2,1)S(1)} %copy-done.74), channel_id=1, source_target_pairs={{0,1},{1,0},{2,3},{3,2},{4,5},{5,4},{6,7},{7,6},{8,9},{9,8},{10,11... | collective-permute-start | bytes 3538952 | tf_op jit(solution)/shard_map/ppermute | solution.py:65
  205.6 85.7 %collective-permute-start.44 = (bf16[512,1152]{1,0:T(8,128)(2,1)S(1)}, bf16[512,1152]{1,0:T(8,128)(2,1)S(1)}, u32[]{:S(2)}, u32[]{:S(2)}) collective-permute-start(bf16[512,1152]{1,0:T(8,128)(2,1)S(1)} %fusion.1), channel_id=1, source_target_pairs={{0,1},{1,0},{2,3},{3,2},{4,5},{5,4},{6,7},{7,6},{8,9},{9,8},{10,11... | collective-permute-start | bytes 3538952 | tf_op jit(solution)/shard_map/ppermute | solution.py:65
  209.4 70.1 %collective-permute-start.25 = (bf16[512,1152]{1,0:T(8,128)(2,1)S(1)}, bf16[512,1152]{1,0:T(8,128)(2,1)S(1)}, u32[]{:S(2)}, u32[]{:S(2)}) collective-permute-start(bf16[512,1152]{1,0:T(8,128)(2,1)S(1)} %fusion.2), channel_id=1, source_target_pairs={{0,1},{1,0},{2,3},{3,2},{4,5},{5,4},{6,7},{7,6},{8,9},{9,8},{10,11... | collective-permute-start | bytes 3538952 | tf_op jit(solution)/shard_map/ppermute | solution.py:65
  230.2 55.0 %collective-permute-start.23 = (bf16[448,1024]{1,0:T(8,128)(2,1)S(1)}, bf16[448,1024]{1,0:T(8,128)(2,1)S(1)}, u32[]{:S(2)}, u32[]{:S(2)}) collective-permute-start(bf16[448,1024]{1,0:T(8,128)(2,1)S(1)} %add_convert_fusion.2), channel_id=1, source_target_pairs={{0,4},{2,6},{4,0},{6,2},{1,5},{3,7},{5,1},{7,3},{8,12},{10,14},{12... | collective-permute-start | bytes 2752520 | tf_op jit(solution)/shard_map/ppermute | solution.py:75
  279.5 30.2 %collective-permute-start.54 = (bf16[1152,512]{1,0:T(8,128)(2,1)S(1)}, bf16[1152,512]{1,0:T(8,128)(2,1)S(1)}, u32[]{:S(2)}, u32[]{:S(2)}) collective-permute-start(bf16[1152,512]{1,0:T(8,128)(2,1)S(1)} %get-tuple-element.203), channel_id=1, source_target_pairs={{0,8},{24,16},{1,9},{25,17},{2,10},{26,18},{3,11},{27,19},{4,12},{... | collective-permute-start | bytes 3538952 | tf_op jit(solution)/shard_map/ppermute | solution.py:86
  286.5 36.9 %collective-permute-start.28 = (bf16[448,1024]{1,0:T(8,128)(2,1)S(1)}, bf16[448,1024]{1,0:T(8,128)(2,1)S(1)}, u32[]{:S(2)}, u32[]{:S(2)}) collective-permute-start(bf16[448,1024]{1,0:T(8,128)(2,1)S(1)} %add_convert_fusion.1), channel_id=1, source_target_pairs={{0,4},{2,6},{4,0},{6,2},{1,5},{3,7},{5,1},{7,3},{8,12},{10,14},{12... | collective-permute-start | bytes 2752520 | tf_op jit(solution)/shard_map/ppermute | solution.py:75
  295.3 69.3 %collective-permute-start.45 = (bf16[512,1152]{1,0:T(8,128)(2,1)}, bf16[512,1152]{1,0:T(8,128)(2,1)S(1)}, u32[]{:S(2)}, u32[]{:S(2)}) collective-permute-start(bf16[512,1152]{1,0:T(8,128)(2,1)} %get-tuple-element.201), channel_id=1, source_target_pairs={{0,8},{24,16},{1,9},{25,17},{2,10},{26,18},{3,11},{27,19},{4,12},{... | collective-permute-start | bytes 3538952 | tf_op jit(solution)/shard_map/ppermute | solution.py:86
  311.8 23.0 %collective-permute-start.55 = (bf16[1152,512]{1,0:T(8,128)(2,1)S(1)}, bf16[1152,512]{1,0:T(8,128)(2,1)}, u32[]{:S(2)}, u32[]{:S(2)}) collective-permute-start(bf16[1152,512]{1,0:T(8,128)(2,1)S(1)} %fusion.51), channel_id=1, source_target_pairs={{8,16},{16,8},{9,17},{17,9},{10,18},{18,10},{11,19},{19,11},{12,20... | collective-permute-start | bytes 3538952 | tf_op jit(solution)/shard_map/ppermute | solution.py:90
  313.5 44.7 %collective-permute-start.49 = (bf16[512,1152]{1,0:T(8,128)(2,1)S(1)}, bf16[512,1152]{1,0:T(8,128)(2,1)S(1)}, u32[]{:S(2)}, u32[]{:S(2)}) collective-permute-start(bf16[512,1152]{1,0:T(8,128)(2,1)S(1)} %get-tuple-element.138), channel_id=1, source_target_pairs={{0,8},{24,16},{1,9},{25,17},{2,10},{26,18},{3,11},{27,19},{4,12},{... | collective-permute-start | bytes 3538952 | tf_op jit(solution)/shard_map/ppermute | solution.py:86
  328.4 30.9 %collective-permute-start.39 = (bf16[256,1024]{1,0:T(8,128)(2,1)S(1)}, bf16[256,1024]{1,0:T(8,128)(2,1)S(1)}, u32[]{:S(2)}, u32[]{:S(2)}) collective-permute-start(bf16[256,1024]{1,0:T(8,128)(2,1)S(1)} %convolution_convert_fusion.4), channel_id=1, source_target_pairs={{0,2},{2,0},{4,6},{6,4},{1,3},{3,1},{5,7},{7,5},{8,10},{10,8},{12,... | collective-permute-start | bytes 1572872 | tf_op jit(solution)/shard_map/ppermute | solution.py:70
  334.4 27.0 %collective-permute-start.30 = (bf16[3,1024,256]{1,2,0:T(8,128)(2,1)S(1)}, bf16[3,1024,256]{1,2,0:T(8,128)(2,1)S(1)}, u32[]{:S(2)}, u32[]{:S(2)}) collective-permute-start(bf16[3,1024,256]{1,2,0:T(8,128)(2,1)S(1)} %fusion.46), channel_id=1, source_target_pairs={{0,2},{2,0},{4,6},{6,4},{1,3},{3,1},{5,7},{7,5},{8,10},{10,8},{12,... | collective-permute-start | bytes 4718600 | tf_op jit(solution)/shard_map/ppermute | solution.py:70
  337.3 80.3 %collective-permute-start.56 = (bf16[1152,512]{1,0:T(8,128)(2,1)S(1)}, bf16[1152,512]{1,0:T(8,128)(2,1)S(1)}, u32[]{:S(2)}, u32[]{:S(2)}) collective-permute-start(bf16[1152,512]{1,0:T(8,128)(2,1)S(1)} %reduce-precision_convert_fusion), channel_id=1, source_target_pairs={{8,0},{16,24},{9,1},{17,25},{10,2},{18,26},{11,3},{19,27},{12,4},{... | collective-permute-start | bytes 3538952 | tf_op jit(solution)/shard_map/ppermute | solution.py:97
  362.4 23.5 %collective-permute-start.37 = (bf16[3,512,256]{1,2,0:T(8,128)(2,1)S(1)}, bf16[3,512,256]{1,2,0:T(8,128)(2,1)S(1)}, u32[]{:S(2)}, u32[]{:S(2)}) collective-permute-start(bf16[3,512,256]{1,2,0:T(8,128)(2,1)S(1)} %fusion.41), channel_id=1, source_target_pairs={{0,1},{1,0},{2,3},{3,2},{4,5},{5,4},{6,7},{7,6},{8,9},{9,8},{10,11... | collective-permute-start | bytes 2359304 | tf_op jit(solution)/shard_map/ppermute | solution.py:65
  364.6 37.6 %collective-permute-start.33 = (bf16[896,512]{1,0:T(8,128)(2,1)S(1)}, bf16[896,512]{1,0:T(8,128)(2,1)S(1)}, u32[]{:S(2)}, u32[]{:S(2)}) collective-permute-start(bf16[896,512]{1,0:T(8,128)(2,1)S(1)} %bitcast_convert_fusion), channel_id=1, source_target_pairs={{0,4},{2,6},{4,0},{6,2},{1,5},{3,7},{5,1},{7,3},{8,12},{10,14},{12... | collective-permute-start | bytes 2752520 | tf_op jit(solution)/shard_map/ppermute | solution.py:75
  368.9 58.9 %collective-permute-start.46 = (bf16[512,1152]{1,0:T(8,128)(2,1)S(1)}, bf16[512,1152]{1,0:T(8,128)(2,1)S(1)}, u32[]{:S(2)}, u32[]{:S(2)}) collective-permute-start(bf16[512,1152]{1,0:T(8,128)(2,1)S(1)} %fusion.49), channel_id=1, source_target_pairs={{8,16},{16,8},{9,17},{17,9},{10,18},{18,10},{11,19},{19,11},{12,20... | collective-permute-start | bytes 3538952 | tf_op jit(solution)/shard_map/ppermute | solution.py:90
  370.0 29.8 %collective-permute-start.32 = (bf16[1792,128]{1,0:T(8,128)(2,1)S(1)}, bf16[1792,128]{1,0:T(8,128)(2,1)S(1)}, u32[]{:S(2)}, u32[]{:S(2)}) collective-permute-start(bf16[1792,128]{1,0:T(8,128)(2,1)S(1)} %get-tuple-element.163), channel_id=1, source_target_pairs={{0,1},{1,0},{2,3},{3,2},{4,5},{5,4},{6,7},{7,6},{8,9},{9,8},{10,11... | collective-permute-start | bytes 1376264 | tf_op jit(solution)/shard_map/ppermute | solution.py:65
  385.9 31.6 %collective-permute-start.41 = (bf16[256,512]{1,0:T(8,128)(2,1)S(1)}, bf16[256,512]{1,0:T(8,128)(2,1)S(1)}, u32[]{:S(2)}, u32[]{:S(2)}) collective-permute-start(bf16[256,512]{1,0:T(8,128)(2,1)S(1)} %get-tuple-element.199), channel_id=1, source_target_pairs={{0,8},{24,16},{1,9},{25,17},{2,10},{26,18},{3,11},{27,19},{4,12},{... | collective-permute-start | bytes 786440 | tf_op jit(solution)/shard_map/ppermute | solution.py:86
  399.8 38.2 %collective-permute-start.51 = (bf16[512,1152]{1,0:T(8,128)(2,1)S(1)}, bf16[512,1152]{1,0:T(8,128)(2,1)S(1)}, u32[]{:S(2)}, u32[]{:S(2)}) collective-permute-start(bf16[512,1152]{1,0:T(8,128)(2,1)S(1)} %reduce-precision_convert_fusion.2), channel_id=1, source_target_pairs={{8,0},{16,24},{9,1},{17,25},{10,2},{18,26},{11,3},{19,27},{12,4},{... | collective-permute-start | bytes 3538952 | tf_op jit(solution)/shard_map/ppermute | solution.py:97
  407.8 28.1 %collective-permute-start.38 = (bf16[3,512,256]{1,2,0:T(8,128)(2,1)S(1)}, bf16[3,512,256]{1,2,0:T(8,128)(2,1)S(1)}, u32[]{:S(2)}, u32[]{:S(2)}) collective-permute-start(bf16[3,512,256]{1,2,0:T(8,128)(2,1)S(1)} %get-tuple-element.197), channel_id=1, source_target_pairs={{0,8},{24,16},{1,9},{25,17},{2,10},{26,18},{3,11},{27,19},{4,12},{... | collective-permute-start | bytes 2359304 | tf_op jit(solution)/shard_map/ppermute | solution.py:86
  427.8 24.1 %collective-permute-start.60 = (f32[5,1024]{1,0:T(8,128)S(1)}, f32[5,1024]{1,0:T(8,128)S(1)}, u32[]{:S(2)}, u32[]{:S(2)}) collective-permute-start(f32[5,1024]{1,0:T(8,128)S(1)} %add.381), channel_id=1, source_target_pairs={{0,8},{24,16},{1,9},{25,17},{2,10},{26,18},{3,11},{27,19},{4,12},{... | collective-permute-start | bytes 61448 | tf_op jit(solution)/shard_map/ppermute | solution.py:86
  432.8 30.7 %collective-permute-start.52 = (bf16[512,1152]{1,0:T(8,128)(2,1)S(1)}, bf16[512,1152]{1,0:T(8,128)(2,1)S(1)}, u32[]{:S(2)}, u32[]{:S(2)}) collective-permute-start(bf16[512,1152]{1,0:T(8,128)(2,1)S(1)} %reduce-precision_convert_fusion.4), channel_id=1, source_target_pairs={{8,0},{16,24},{9,1},{17,25},{10,2},{18,26},{11,3},{19,27},{12,4},{... | collective-permute-start | bytes 3538952 | tf_op jit(solution)/shard_map/ppermute | solution.py:97
  434.2 34.9 %collective-permute-start.48 = (bf16[256,512]{1,0:T(8,128)(2,1)S(1)}, bf16[256,512]{1,0:T(8,128)(2,1)S(1)}, u32[]{:S(2)}, u32[]{:S(2)}) collective-permute-start(bf16[256,512]{1,0:T(8,128)(2,1)S(1)} %reduce-precision_convert_fusion.8), channel_id=1, source_target_pairs={{8,0},{16,24},{9,1},{17,25},{10,2},{18,26},{11,3},{19,27},{12,4},{... | collective-permute-start | bytes 786440 | tf_op jit(solution)/shard_map/ppermute | solution.py:97
  450.7 36.4 %collective-permute-start.47 = (bf16[3,512,256]{1,2,0:T(8,128)(2,1)S(1)}, bf16[3,512,256]{1,2,0:T(8,128)(2,1)S(1)}, u32[]{:S(2)}, u32[]{:S(2)}) collective-permute-start(bf16[3,512,256]{1,2,0:T(8,128)(2,1)S(1)} %reduce-precision_convert_fusion.6), channel_id=1, source_target_pairs={{8,0},{16,24},{9,1},{17,25},{10,2},{18,26},{11,3},{19,27},{12,4},{... | collective-permute-start | bytes 2359304 | tf_op jit(solution)/shard_map/ppermute | solution.py:97
  (117 other events, 942.7 us)
